TPU v7x, 32 devices: a whole 2x2x4 slice. The times are simulated.
32 devices in a mesh: parts: 2 (over y), blk: 4 (over z), row: 2 (over x), sub: 2 (over core).
Axes of the slice: x: 2, y: 2, z: 4, core: 2. Of those that a mesh axis runs over, the one named last changes fastest.
Arguments:
- query_grads: bfloat16 [512, 4, 2048], P('blk', None, 'sub'), may hold values from -6 to 6
- curvature: bfloat16 [4, 2048, 2048], P('blk', ('row', 'sub')), may hold values from -0.125 to 0.125
- train_grads: bfloat16 [5120, 4, 2048], P(('parts', 'row', 'sub'), 'blk'), parts along dimension 0, may hold values from -0.0625 to 0.0625
- query_ids: int32 [1024], P('parts'), parts along dimension 0, may hold values from 0 to 511, each once
- block_map: int32 [4], replicated, may hold values from 0 to 3, each once
- row_ids: int32 [5120], P(('parts', 'row', 'sub')), parts along dimension 0, may hold values from 0 to 639
Outputs:
- scores: float32 [512, 5120], P('blk', ('parts', 'row', 'sub')), parts along dimension 1
There are 2 independent parts, one for each index of `parts`. A program takes and returns all parts, laid end to end along the dimension named above; an argument that names none is the same for every part. Nothing has to cross between parts.
Inputs may be any that keep to these rules, and one draw needn't show every extreme that they name: `query_ids`: each value appears once. `block_map`: each value appears once.
All inputs are finite; a program needn't handle non-finite values.
Results may differ from a plain program's by a relative error of at most 0.0029.
Values may be sent and summed in bfloat16 or wider, within the bound.
No kernel may reach another device: no remote copies, remote signals or barrier semaphores. Data moves between devices by JAX's collectives and lax.ppermute only.
A program may use at most 64 MiB of HBM per device.

v0:
```python
import jax
import jax.numpy as jnp
from jax import lax
from jax.sharding import PartitionSpec as P


def per_device(query_grads, curvature, train_grads, query_ids, block_map, row_ids):
    mine = jnp.take(query_grads, block_map, axis=1)
    arrived = lax.all_to_all(mine, "blk", split_axis=1, concat_axis=0, tiled=True)
    queries = arrived.shape[0]
    precond = jnp.einsum(
        "qsj,sij->qsi",
        lax.all_gather(arrived, "sub", axis=2, tiled=True),
        curvature,
        preferred_element_type=jnp.float32,
    ).astype(jnp.bfloat16)
    inverse = (
        jnp.zeros((queries,), jnp.int32).at[query_ids].set(jnp.arange(queries, dtype=jnp.int32))
    )
    ordered = jnp.take(precond, inverse, axis=0)
    chosen = jnp.take(train_grads, row_ids, axis=0)
    partial_value = jnp.einsum(
        "qsk,rsk->qr",
        lax.all_gather(ordered, ("row", "sub"), axis=2, tiled=True),
        chosen,
        preferred_element_type=jnp.float32,
    )
    return lax.psum_scatter(partial_value, "blk", scatter_dimension=0, tiled=True)


def solution(mesh):
    placed = (
        P("blk", None, "sub"),
        P("blk", ("row", "sub"), None),
        P(("parts", "row", "sub"), "blk", None),
        P("parts"),
        P(),
        P(("parts", "row", "sub")),
    )
    return jax.shard_map(
        per_device,
        mesh=mesh,
        in_specs=placed,
        out_specs=P("blk", ("parts", "row", "sub")),
        check_vma=False,
    )
```

profile of v0, /device:TPU:0, one launch (start us, length us, event | category | flops | bytes accessed | tf_op | source)
XLA Modules:
  0.0 133.5 jit_solution(11992758323479835850)
XLA Ops:
  6.5 0.0 copy-start
  6.5 0.0 all-gather.3.cloned.1.call-start
  6.5 0.8 compare_and_fusion.1
  7.4 0.7 compare_select_fusion.3
  8.0 6.1 %gather_fusion = bf16[4,128,1024]{2,0,1:T(4,128)(2,1)} fusion(bf16[128,4,1024]{2,1,0:T(4,128)(2,1)} %param.6, s32[1024]{0:T(1024)S(1)} %pad_clamp_fusion.2), kind=kCustom, calls=%fused_computation | custom fusion | bytes 2097168 | tf_op jit(solution)/shard_map/jit(_take)/gather | solution.py:8
  14.1 1.7 %select_bitcast_fusion = bf16[128,4,1024]{2,1,0:T(4,128)(2,1)S(1)} fusion(bf16[4,128,1024]{2,0,1:T(4,128)(2,1)} %gather_fusion, pred[4]{0:T(512)(128)(4,1)S(1)} %compare_and_fusion.1), kind=kLoop, calls=%fused_computation.14 | loop fusion | flops 524288 | bytes 2097156 | tf_op jit(solution)/shard_map/jit(_take)/select_n | solution.py:8
  15.9 0.3 copy.8
  16.2 0.0 copy-start.2
  16.2 32.0 %all_to_all.18 = bf16[128,4,1024]{2,0,1:T(8,128)(2,1)} all-to-all(bf16[128,4,1024]{2,0,1:T(8,128)(2,1)S(1)} %copy.8), channel_id=1, replica_groups=mesh['parts'=2,'blk'=4,'row'=2,'sub'=2] {'blk'}, dimensions={1} | all-to-all | bytes 2097152 | tf_op jit(solution)/shard_map/all_to_all | solution.py:9
  48.2 0.0 all-gather.3.cloned.1.call-update
  48.2 0.0 all-gather.5.cloned.1.call-start
  48.2 0.0 copy-done.2
  48.3 2.4 %scatter_custom_fusion = s32[512]{0:T(512)S(1)} fusion(s32[512]{0:T(512)S(1)} %compare_select_fusion.2, s32[512]{0:T(512)S(1)} %iota.3, s32[]{:T(128)} %constant.30.clone.1), kind=kCustom, calls=%fused_computation.26 | custom fusion | bytes 2052 | tf_op jit(solution)/shard_map/scatter | solution.py:18
  50.8 7.3 %all-gather.3.cloned.1.call-done = bf16[512,1,2048]{2,0,1:T(8,128)(2,1)} async-done(((bf16[512,1,1024]{2,0,1:T(8,128)(2,1)}), bf16[512,1,2048]{2,0,1:T(8,128)(2,1)}) %all-gather.3.cloned.1.call-update) | async-done | bytes 2097168 | tf_op jit(solution)/shard_map/all_gather | solution.py:13
  58.0 3.5 %fusion.8 = bf16[512,512]{1,0:T(8,128)(2,1)S(1)} fusion(bf16[1,512,2048]{2,1,0:T(8,128)(2,1)} %param.7, bf16[512,1,2048]{2,0,1:T(8,128)(2,1)} %all-gather.3.cloned.1.call-done), kind=kOutput, calls=%fused_computation.13 | convolution fusion | flops 1074003968 | bytes 4718592 | tf_op jit(solution)/shard_map/qsj,sij->qsi/dot_general | solution.py:11
  61.5 0.0 copy-start.1
  61.6 2.6 %gather_fusion.1 = bf16[512,512]{1,0:T(8,128)(2,1)} fusion(bf16[512,512]{1,0:T(8,128)(2,1)S(1)} %fusion.8, s32[1024]{0:T(1024)S(1)} %pad_clamp_fusion.1), kind=kCustom, calls=%fused_computation.1 | custom fusion | bytes 1050624 | tf_op jit(solution)/shard_map/jit(_take)/gather | solution.py:20
  64.2 2.0 %bitcast_select_fusion.2 = bf16[512,1,512]{2,0,1:T(8,128)(2,1)} fusion(bf16[512,512]{1,0:T(8,128)(2,1)} %gather_fusion.1, pred[512]{0:T(512)(128)(4,1)S(1)} %compare_and_fusion.2), kind=kLoop, calls=%fused_computation.15 | loop fusion | flops 262144 | bytes 1049088 | tf_op jit(solution)/shard_map/jit(_take)/select_n | solution.py:20
  66.2 0.0 all-gather.5.cloned.1.call-update
  66.2 0.0 reduce-scatter.2.cloned.1.call-start
  66.2 0.0 copy-done.1
  66.3 0.0 copy-done
  66.3 4.1 %gather_fusion.2 = bf16[640,2048]{1,0:T(8,128)(2,1)} fusion(bf16[640,2048]{1,0:T(8,128)(2,1)S(1)} %bitcast.32, s32[1024]{0:T(1024)S(1)} %pad_clamp_fusion), kind=kCustom, calls=%fused_computation.2 | custom fusion | bytes 5245440 | tf_op jit(solution)/shard_map/jit(_take)/gather | solution.py:21
  70.3 19.7 %all-gather.5.cloned.1.call-done = bf16[512,1,2048]{2,0,1:T(8,128)(2,1)} async-done(((bf16[512,1,512]{2,0,1:T(8,128)(2,1)}), bf16[512,1,2048]{2,0,1:T(8,128)(2,1)}) %all-gather.5.cloned.1.call-update) | async-done | bytes 2097168 | tf_op jit(solution)/shard_map/all_gather | solution.py:24
  90.1 5.4 %fusion = f32[512,640]{1,0:T(8,128)} fusion(bf16[640,2048]{1,0:T(8,128)(2,1)} %gather_fusion.2, pred[640]{0:T(1024)(128)(4,1)S(1)} %compare_and_fusion, bf16[512,1,2048]{2,0,1:T(8,128)(2,1)} %all-gather.5.cloned.1.call-done), kind=kOutput, calls=%fused_computation.4 | convolution fusion | flops 1343488000 | bytes 6029952 | tf_op jit(solution)/shard_map/qsk,rsk->qr/dot_general | solution.py:22
  95.5 0.0 reduce-scatter.2.cloned.1.call-update
  95.5 31.5 %reduce-scatter.2.cloned.1.call-done = f32[128,640]{1,0:T(8,128)} async-done(((f32[512,640]{1,0:T(8,128)}), f32[128,640]{1,0:T(8,128)}) %reduce-scatter.2.cloned.1.call-update) | async-done | bytes 327696 | tf_op jit(solution)/shard_map/reduce_scatter | solution.py:28
  (9 shorter events, 0.1 us)
Async XLA Ops:
  6.5 59.7 %copy-start = (bf16[640,1,2048]{2,0,1:T(8,128)(2,1)S(1)}, bf16[640,1,2048]{2,0,1:T(8,128)(2,1)}, u32[]{:S(2)}) copy-start(bf16[640,1,2048]{2,0,1:T(8,128)(2,1)} %param.8) | copy-start | bytes 7864324
  6.5 51.5 %all-gather.3.cloned.1.call-start = ((), (), s32[]{:S(2)}) async-start(), calls=%async_computation.2 | async-start | bytes 3145728 | tf_op jit(solution)/shard_map/all_gather | solution.py:13
  16.2 32.1 %copy-start.2 = (s32[512]{0:T(512)S(1)}, s32[512]{0:T(512)}, u32[]{:S(2)}) copy-start(s32[512]{0:T(512)} %param.9) | copy-start | bytes 6148
  48.2 41.9 %all-gather.5.cloned.1.call-start = ((), (), s32[]{:S(2)}) async-start(), calls=%async_computation.3 | async-start | bytes 2621440 | tf_op jit(solution)/shard_map/all_gather | solution.py:24
  61.5 4.7 %copy-start.1 = (s32[640]{0:T(1024)S(1)}, s32[640]{0:T(1024)}, u32[]{:S(2)}) copy-start(s32[640]{0:T(1024)} %param.11) | copy-start | bytes 7684
  66.2 60.8 %reduce-scatter.2.cloned.1.call-start = ((), (), s32[]{:S(2)}) async-start(), calls=%async_computation.4 | async-start | bytes 1638400 | tf_op jit(solution)/shard_map/reduce_scatter | solution.py:28
Sparse Core Ops, SparseCore 0:
  48.3 9.6 all-gather.2
  66.3 23.7 all-gather.4
  95.6 31.3 reduce-scatter.1
where the time goes:
time: 134 us
  waiting for transfers between devices  58.6 us (44%)
  blocking collectives  32 us (24%)
  local copies, waits for them, and re-layouts  15.6 us (12%)
  between operations  13.2 us (10%)
  matrix products  8.89 us (7%)
  other arithmetic  5.23 us (4%)
    all_to_all x1, blocking collectives, per_device(): lax.all_to_all(mine, 'blk', split_axis=1, concat_axis=0, tiled=True)  32 us
    reduce_scatter x1, waiting for transfers between devices, per_device(): lax.psum_scatter(partial_value, 'blk', scatter_dimension=0, tiled=True)  31.5 us
    all_gather x1, waiting for transfers between devices, per_device(): lax.all_gather(ordered, ('row', 'sub'), axis=2, tiled=True)  19.7 us
    all_gather x1, waiting for transfers between devices, per_device(): lax.all_gather(arrived, 'sub', axis=2, tiled=True)  7.27 us
    gather x1, local copies, waits for them, and re-layouts, per_device(): mine = jnp.take(query_grads, block_map, axis=1)  6.1 us
    dot_general x1, matrix products, per_device(): jnp.einsum('qsk,rsk->qr', lax.all_gather(ordered, ('row', 'sub'), axis=2,...  5.39 us
    gather x1, local copies, waits for them, and re-layouts, per_device(): chosen = jnp.take(train_grads, row_ids, axis=0)  4.06 us
    dot_general x1, matrix products, per_device(): jnp.einsum('qsj,sij->qsi', lax.all_gather(arrived, 'sub', axis=2, tiled=T...  3.5 us
  transfers between devices with their start and end apart: 3, of which 3 were waited for; matrix products, arithmetic and copies ran while one was open for 5% of the time, Pallas kernels for 0%

commit v1 on v0

--- a/solution.py
+++ b/solution.py
@@ -4,9 +4,15 @@
 from jax.sharding import PartitionSpec as P
 
 
+def exchange_blocks(x, name, split, join):
+    pieces = jnp.split(x, lax.axis_size(name), axis=split)
+    got = lax.all_to_all(jnp.stack(pieces), name, 0, 0)
+    return jnp.concatenate(got, axis=join)
+
+
 def per_device(query_grads, curvature, train_grads, query_ids, block_map, row_ids):
     mine = jnp.take(query_grads, block_map, axis=1)
-    arrived = lax.all_to_all(mine, "blk", split_axis=1, concat_axis=0, tiled=True)
+    arrived = exchange_blocks(mine, "blk", 1, 0)
     queries = arrived.shape[0]
     precond = jnp.einsum(
         "qsj,sij->qsi",

time: 134 us -> 136 us (1.015)
  local copies, waits for them, and re-layouts: 15.6 us -> 17.2 us
    split x0 -> x1, local copies, waits for them, and re-layouts: none -> 1.55 us  [exchange_blocks(): pieces = jnp.split(x, lax.axis_size(name), axis=split)]
where the time goes in v1:
time: 136 us; the launch traced here: 135 us
  waiting for transfers between devices  58.5 us (43%)
  blocking collectives  32 us (24%)
  local copies, waits for them, and re-layouts  17.2 us (13%)
  between operations  13.2 us (10%)
  matrix products  8.89 us (7%)
  other arithmetic  5.37 us (4%)
    all_to_all x1, blocking collectives, exchange_blocks(): got = lax.all_to_all(jnp.stack(pieces), name, 0, 0)  32 us
    reduce_scatter x1, waiting for transfers between devices, per_device(): lax.psum_scatter(partial_value, 'blk', scatter_dimension=0, tiled=True)  31.5 us
    all_gather x1, waiting for transfers between devices, per_device(): lax.all_gather(ordered, ('row', 'sub'), axis=2, tiled=True)  19.7 us
    all_gather x1, waiting for transfers between devices, per_device(): lax.all_gather(arrived, 'sub', axis=2, tiled=True)  7.27 us
    gather x1, local copies, waits for them, and re-layouts, per_device(): mine = jnp.take(query_grads, block_map, axis=1)  6.11 us
    dot_general x1, matrix products, per_device(): jnp.einsum('qsk,rsk->qr', lax.all_gather(ordered, ('row', 'sub'), axis=2,...  5.38 us
    gather x1, local copies, waits for them, and re-layouts, per_device(): chosen = jnp.take(train_grads, row_ids, axis=0)  4.08 us
    dot_general x1, matrix products, per_device(): jnp.einsum('qsj,sij->qsi', lax.all_gather(arrived, 'sub', axis=2, tiled=T...  3.5 us
  transfers between devices with their start and end apart: 3, of which 3 were waited for; matrix products, arithmetic and copies ran while one was open for 5% of the time, Pallas kernels for 0%

profile of v1, /device:TPU:0, one launch (start us, length us, event | category | flops | bytes accessed | tf_op | source)
XLA Modules:
  0.0 135.3 jit_solution(17756930626297761209)
XLA Ops:
  6.5 0.0 copy-start
  6.5 0.0 all-gather.3.cloned.1.call-start
  6.5 0.8 compare_and_fusion.1
  7.4 0.7 compare_select_fusion.3
  8.0 6.1 %gather_fusion = bf16[4,128,1024]{2,0,1:T(4,128)(2,1)} fusion(bf16[128,4,1024]{2,1,0:T(4,128)(2,1)} %param.6, s32[1024]{0:T(1024)S(1)} %pad_clamp_fusion.2), kind=kCustom, calls=%fused_computation | custom fusion | bytes 2097168 | tf_op jit(solution)/shard_map/jit(_take)/gather | solution.py:14
  14.1 1.7 %select_bitcast_fusion = bf16[128,4,1024]{2,1,0:T(4,128)(2,1)S(1)} fusion(bf16[4,128,1024]{2,0,1:T(4,128)(2,1)} %gather_fusion, pred[4]{0:T(512)(128)(4,1)S(1)} %compare_and_fusion.1), kind=kLoop, calls=%fused_computation.15 | loop fusion | flops 524288 | bytes 2097156 | tf_op jit(solution)/shard_map/jit(_take)/select_n | solution.py:14
  15.9 1.6 %fusion.16 = (bf16[128,1,1024]{2,1,0:T(2,128)(2,1)S(1)}, bf16[128,1,1024]{2,1,0:T(2,128)(2,1)S(1)}, bf16[128,1,1024]{2,1,0:T(2,128)(2,1)S(1)}, bf16[128,1,1024]{2,1,0:T(2,128)(2,1)S(1)}) fusion(bf16[128,4,1024]{2,1,0:T(4,128)(2,1)S(1)} %select_bitcast_fusion), kind=kLoop, calls=%fused_computation.34 | loop fusion | bytes 2097152 | tf_op jit(solution)/shard_map/split | solution.py:8
  17.4 0.2 copy_bitcast_fusion.2
  17.6 0.2 copy_bitcast_fusion
  17.8 0.1 pad_maximum_fusion
  17.9 0.0 copy-start.2
  17.9 32.0 %all_to_all.5 = bf16[4,128,1,1024]{3,1,2,0:T(8,128)(2,1)} all-to-all(bf16[4,128,1,1024]{3,1,2,0:T(8,128)(2,1)S(1)} %pad_maximum_fusion), channel_id=1, replica_groups=mesh['parts'=2,'blk'=4,'row'=2,'sub'=2] {'blk'}, dimensions={0} | all-to-all | bytes 2097152 | tf_op jit(solution)/shard_map/all_to_all | solution.py:9
  49.9 0.0 all-gather.3.cloned.1.call-update
  49.9 0.0 all-gather.5.cloned.1.call-start
  50.0 0.0 copy-done.2
  50.0 2.4 %scatter_custom_fusion = s32[512]{0:T(512)S(1)} fusion(s32[512]{0:T(512)S(1)} %compare_select_fusion.2, s32[512]{0:T(512)S(1)} %iota.3, s32[]{:T(128)} %constant.30.clone.1), kind=kCustom, calls=%fused_computation.31 | custom fusion | bytes 2052 | tf_op jit(solution)/shard_map/scatter | solution.py:24
  52.5 7.3 %all-gather.3.cloned.1.call-done = bf16[512,1,2048]{2,0,1:T(8,128)(2,1)} async-done(((bf16[512,1,1024]{2,0,1:T(8,128)(2,1)}), bf16[512,1,2048]{2,0,1:T(8,128)(2,1)}) %all-gather.3.cloned.1.call-update) | async-done | bytes 2097168 | tf_op jit(solution)/shard_map/all_gather | solution.py:19
  59.8 3.5 %fusion.8 = bf16[512,512]{1,0:T(8,128)(2,1)S(1)} fusion(bf16[1,512,2048]{2,1,0:T(8,128)(2,1)} %param.7, bf16[512,1,2048]{2,0,1:T(8,128)(2,1)} %all-gather.3.cloned.1.call-done), kind=kOutput, calls=%fused_computation.13 | convolution fusion | flops 1074003968 | bytes 4718592 | tf_op jit(solution)/shard_map/qsj,sij->qsi/dot_general | solution.py:17
  63.3 0.0 copy-start.1
  63.3 2.6 %gather_fusion.1 = bf16[512,512]{1,0:T(8,128)(2,1)} fusion(bf16[512,512]{1,0:T(8,128)(2,1)S(1)} %fusion.8, s32[1024]{0:T(1024)S(1)} %pad_clamp_fusion.1), kind=kCustom, calls=%fused_computation.1 | custom fusion | bytes 1050624 | tf_op jit(solution)/shard_map/jit(_take)/gather | solution.py:26
  65.9 2.0 %bitcast_select_fusion.2 = bf16[512,1,512]{2,0,1:T(8,128)(2,1)} fusion(bf16[512,512]{1,0:T(8,128)(2,1)} %gather_fusion.1, pred[512]{0:T(512)(128)(4,1)S(1)} %compare_and_fusion.2), kind=kLoop, calls=%fused_computation.16 | loop fusion | flops 262144 | bytes 1049088 | tf_op jit(solution)/shard_map/jit(_take)/select_n | solution.py:26
  67.9 0.0 all-gather.5.cloned.1.call-update
  67.9 0.0 reduce-scatter.2.cloned.1.call-start
  68.0 0.0 copy-done.1
  68.0 0.0 copy-done
  68.0 4.1 %gather_fusion.2 = bf16[640,2048]{1,0:T(8,128)(2,1)} fusion(bf16[640,2048]{1,0:T(8,128)(2,1)S(1)} %bitcast.36, s32[1024]{0:T(1024)S(1)} %pad_clamp_fusion), kind=kCustom, calls=%fused_computation.2 | custom fusion | bytes 5245440 | tf_op jit(solution)/shard_map/jit(_take)/gather | solution.py:27
  72.1 19.7 %all-gather.5.cloned.1.call-done = bf16[512,1,2048]{2,0,1:T(8,128)(2,1)} async-done(((bf16[512,1,512]{2,0,1:T(8,128)(2,1)}), bf16[512,1,2048]{2,0,1:T(8,128)(2,1)}) %all-gather.5.cloned.1.call-update) | async-done | bytes 2097168 | tf_op jit(solution)/shard_map/all_gather | solution.py:30
  91.8 5.4 %fusion = f32[512,640]{1,0:T(8,128)} fusion(bf16[640,2048]{1,0:T(8,128)(2,1)} %gather_fusion.2, pred[640]{0:T(1024)(128)(4,1)S(1)} %compare_and_fusion, bf16[512,1,2048]{2,0,1:T(8,128)(2,1)} %all-gather.5.cloned.1.call-done), kind=kOutput, calls=%fused_computation.4 | convolution fusion | flops 1343488000 | bytes 6029952 | tf_op jit(solution)/shard_map/qsk,rsk->qr/dot_general | solution.py:28
  97.2 0.0 reduce-scatter.2.cloned.1.call-update
  97.2 31.5 %reduce-scatter.2.cloned.1.call-done = f32[128,640]{1,0:T(8,128)} async-done(((f32[512,640]{1,0:T(8,128)}), f32[128,640]{1,0:T(8,128)}) %reduce-scatter.2.cloned.1.call-update) | async-done | bytes 327696 | tf_op jit(solution)/shard_map/reduce_scatter | solution.py:34
  (9 shorter events, 0.1 us)
Async XLA Ops:
  6.5 61.5 %copy-start = (bf16[640,1,2048]{2,0,1:T(8,128)(2,1)S(1)}, bf16[640,1,2048]{2,0,1:T(8,128)(2,1)}, u32[]{:S(2)}) copy-start(bf16[640,1,2048]{2,0,1:T(8,128)(2,1)} %param.8) | copy-start | bytes 7864324
  6.5 53.2 %all-gather.3.cloned.1.call-start = ((), (), s32[]{:S(2)}) async-start(), calls=%async_computation.2 | async-start | bytes 3145728 | tf_op jit(solution)/shard_map/all_gather | solution.py:19
  17.9 32.1 %copy-start.2 = (s32[512]{0:T(512)S(1)}, s32[512]{0:T(512)}, u32[]{:S(2)}) copy-start(s32[512]{0:T(512)} %param.9) | copy-start | bytes 6148
  49.9 41.9 %all-gather.5.cloned.1.call-start = ((), (), s32[]{:S(2)}) async-start(), calls=%async_computation.3 | async-start | bytes 2621440 | tf_op jit(solution)/shard_map/all_gather | solution.py:30
  63.3 4.7 %copy-start.1 = (s32[640]{0:T(1024)S(1)}, s32[640]{0:T(1024)}, u32[]{:S(2)}) copy-start(s32[640]{0:T(1024)} %param.11) | copy-start | bytes 7684
  67.9 60.8 %reduce-scatter.2.cloned.1.call-start = ((), (), s32[]{:S(2)}) async-start(), calls=%async_computation.4 | async-start | bytes 1638400 | tf_op jit(solution)/shard_map/reduce_scatter | solution.py:34
Sparse Core Ops, SparseCore 0:
  50.1 9.6 all-gather.2
  68.0 23.7 all-gather.4
  97.3 31.3 reduce-scatter.1
